TPU v7x, 512 devices: a whole 4x8x8 slice. The times are simulated.
512 devices in a mesh: dp: 128 (over y, z, core), shard: 4 (over x).
Axes of the slice: x: 4, y: 8, z: 8, core: 2. Of those that a mesh axis runs over, the one named last changes fastest.
Arguments:
- acts: bfloat16 [131072, 1792], P('dp', 'shard'), may hold values from -6 to 6
- grad_out: bfloat16 [131072, 3584], P('dp', 'shard'), may hold values from -0.016479492 to 0.016479492
- projector: bfloat16 [1792, 256], P('shard'), may hold values from -6 to 6
- moment: bfloat16 [256, 3584], P(None, 'shard'), may hold values from -4 to 4
- second: bfloat16 [256, 3584], P(None, 'shard'), may hold values from 0.29882812 to 3
Outputs:
- new_projector: bfloat16 [1792, 256], P('shard')
- new_moment: bfloat16 [256, 3584], P(None, 'shard')
- new_second: bfloat16 [256, 3584], P(None, 'shard')
- weight_update: bfloat16 [1792, 3584], P('dp', 'shard')
All inputs are finite; a program needn't handle non-finite values.
Results may differ from a plain program's by a relative error of at most 0.0055.
Values may be sent and summed in bfloat16 or wider, within the bound.
A program may use at most 64 MiB of HBM per device.

v0:
```python
import jax
import jax.numpy as jnp
from jax import lax
from jax.sharding import PartitionSpec as P

D = 1792
RANK = 256


def shards(acts, grad_out, projector, moment, second):
    inv_width = 1.0 / D**0.5
    partial_value = jnp.dot(acts, projector, preferred_element_type=jnp.float32)
    summed = lax.psum(partial_value, "shard")
    proj_acts = (summed * inv_width).astype(jnp.bfloat16)
    local_grad = jnp.einsum("tr,tf->rf", proj_acts, grad_out, preferred_element_type=jnp.float32)
    proj_grad = lax.psum(local_grad, "dp")
    proj_low = proj_grad.astype(jnp.bfloat16)
    score_terms = jnp.einsum("tf,rf->tr", grad_out, proj_low, preferred_element_type=jnp.float32)
    token_scores = lax.psum(score_terms, "shard").astype(jnp.bfloat16)
    local_sub = jnp.einsum("td,tr->dr", acts, token_scores, preferred_element_type=jnp.float32)
    subspace = lax.psum(local_sub, "dp")
    gram_local = jnp.dot(
        subspace.T, subspace, precision=lax.Precision.HIGHEST, preferred_element_type=jnp.float32
    )
    gram_matrix = lax.psum(gram_local, "shard")
    mean_square = jnp.trace(gram_matrix) / (D * RANK) + 1e-06
    cubic = jnp.dot(
        subspace, gram_matrix, precision=lax.Precision.HIGHEST, preferred_element_type=jnp.float32
    )
    new_projector = (
        (1.5 * subspace - 0.5 * cubic / (mean_square * D)) / jnp.sqrt(mean_square)
    ).astype(jnp.bfloat16)
    moment_f = 0.9 * moment.astype(jnp.float32) + 0.1 * proj_grad
    second_f = 0.95 * second.astype(jnp.float32) + 0.05 * proj_grad * proj_grad
    first_fix = 1.0 - 0.9**20
    second_fix = 1.0 - 0.95**20
    direction = (moment_f / first_fix / (jnp.sqrt(second_f / second_fix) + 1e-08)).astype(
        jnp.bfloat16
    )
    row_count = D // lax.axis_size("dp")
    replica = lax.axis_index("dp")
    all_rows = lax.all_gather(projector, "shard", axis=0, tiled=True)
    own_rows = lax.dynamic_slice_in_dim(all_rows, replica * row_count, row_count, 0)
    weight_update = (
        jnp.dot(own_rows, direction, preferred_element_type=jnp.float32) / RANK**0.5
    ).astype(jnp.bfloat16)
    return (
        new_projector,
        moment_f.astype(jnp.bfloat16),
        second_f.astype(jnp.bfloat16),
        weight_update,
    )


def solution(mesh):
    in_specs = (
        P("dp", "shard"),
        P("dp", "shard"),
        P("shard", None),
        P(None, "shard"),
        P(None, "shard"),
    )
    out_specs = (P("shard", None), P(None, "shard"), P(None, "shard"), P("dp", "shard"))
    return jax.shard_map(shards, mesh=mesh, in_specs=in_specs, out_specs=out_specs, check_vma=False)
```

profile of v0, /device:TPU:8, one launch (start us, length us, event | category | flops | bytes accessed | tf_op | source)
XLA Modules:
  0.0 563.3 jit_solution(5339090869765811914)
XLA Ops:
  7.2 0.0 copy-start
  7.2 0.0 all-reduce.6.cloned.1.call-start
  7.2 2.9 fusion.22
  10.1 0.0 all-reduce.6.cloned.1.call-update
  10.1 0.0 copy-start.3
  10.1 0.0 all-reduce.8.cloned.1.call-start
  10.2 61.5 %all-reduce.6.cloned.1.call-done = f32[1024,256]{1,0:T(8,128)} async-done(((f32[1024,256]{1,0:T(8,128)}), f32[1024,256]{1,0:T(8,128)}) %all-reduce.6.cloned.1.call-update) | async-done | bytes 1048592 | tf_op jit(solution)/shard_map/psum | solution.py:13
  71.7 0.0 copy-done
  71.7 2.9 fusion.7
  74.6 0.0 all-reduce.8.cloned.1.call-update
  74.7 0.0 all-reduce.10.cloned.1.call-start
  74.7 0.0 copy-done.3
  74.7 15.0 %all_gather.3 = bf16[1792,256]{1,0:T(8,128)(2,1)} all-gather(bf16[448,256]{1,0:T(8,128)(2,1)S(1)} %copy-done.3), channel_id=1, replica_groups=mesh['dp'=128,'shard'=4] {'shard'}, dimensions={0}, use_global_device_ids=true | all-gather | bytes 1146880 | tf_op jit(solution)/shard_map/all_gather | solution.py:42
  89.8 183.2 %all-reduce.8.cloned.1.call-done = f32[256,896]{1,0:T(8,128)} async-done(((f32[256,896]{1,0:T(8,128)}), f32[256,896]{1,0:T(8,128)}) %all-reduce.8.cloned.1.call-update) | async-done | bytes 917520 | tf_op jit(solution)/shard_map/psum | solution.py:16
  273.0 1.9 convolution_bitcast_fusion
  274.9 33.3 %all-reduce.13 = bf16[1024,256]{0,1:T(8,128)(2,1)S(1)} all-reduce(f32[1024,256]{0,1:T(8,128)S(1)} %convolution_bitcast_fusion), channel_id=1, replica_groups=mesh['dp'=128,'shard'=4] {'shard'}, use_global_device_ids=true, to_apply=%region_2.0 | all-reduce | flops 262144 | bytes 1572864 | tf_op jit(solution)/shard_map/psum | solution.py:19
  308.2 0.0 copy-start.1
  308.2 2.5 convolution_bitcast_fusion.1
  310.7 0.0 all-reduce.10.cloned.1.call-update
  310.7 0.0 all-reduce.12.cloned.1.call-start
  310.8 0.0 copy-done.1
  310.8 2.6 fusion.4
  313.4 186.1 %all-reduce.10.cloned.1.call-done = f32[448,256]{1,0:T(8,128)} async-done(((f32[448,256]{1,0:T(8,128)}), f32[448,256]{1,0:T(8,128)}) %all-reduce.10.cloned.1.call-update) | async-done | bytes 458768 | tf_op jit(solution)/shard_map/psum | solution.py:21
  499.4 2.9 fusion.23
  502.3 0.0 copy-start.2
  502.3 0.0 all-reduce.12.cloned.1.call-update
  502.3 2.4 fusion.10
  504.8 47.5 %all-reduce.12.cloned.1.call-done = f32[256,256]{1,0:T(8,128)} async-done(((f32[256,256]{1,0:T(8,128)}), f32[256,256]{1,0:T(8,128)}) %all-reduce.12.cloned.1.call-update) | async-done | bytes 262160 | tf_op jit(solution)/shard_map/psum | solution.py:25
  552.2 1.6 select_reduce_fusion
  554.5 0.0 copy-done.2
  554.5 2.2 fusion.3
Async XLA Ops:
  7.2 64.6 %copy-start = (bf16[1024,896]{1,0:T(8,128)(2,1)S(1)}, bf16[1024,896]{1,0:T(8,128)(2,1)}, u32[]{:S(2)}) copy-start(bf16[1024,896]{1,0:T(8,128)(2,1)} %param.6) | copy-start | bytes 5505028
  7.2 64.5 %all-reduce.6.cloned.1.call-start = ((), (), s32[]{:S(2)}) async-start(), calls=%async_computation | async-start | bytes 2097152 | tf_op jit(solution)/shard_map/psum | solution.py:13
  10.1 64.6 %copy-start.3 = (bf16[448,256]{1,0:T(8,128)(2,1)S(1)}, bf16[448,256]{1,0:T(8,128)(2,1)}, u32[]{:S(2)}) copy-start(bf16[448,256]{1,0:T(8,128)(2,1)} %param.7) | copy-start | bytes 688132
  10.1 262.9 %all-reduce.8.cloned.1.call-start = ((), (), s32[]{:S(2)}) async-start(), calls=%async_computation.1 | async-start | bytes 1835008 | tf_op jit(solution)/shard_map/psum | solution.py:16
  74.7 424.8 %all-reduce.10.cloned.1.call-start = ((), (), s32[]{:S(2)}) async-start(), calls=%async_computation.2 | async-start | bytes 917504 | tf_op jit(solution)/shard_map/psum | solution.py:21
  308.2 2.6 copy-start.1
  310.7 241.5 %all-reduce.12.cloned.1.call-start = ((), (), s32[]{:S(2)}) async-start(), calls=%async_computation.3 | async-start | bytes 524288 | tf_op jit(solution)/shard_map/psum | solution.py:25
  502.3 52.2 %copy-start.2 = (f32[448,256]{1,0:T(8,128)S(1)}, f32[448,256]{1,0:T(8,128)}, u32[]{:S(2)}) copy-start(f32[448,256]{1,0:T(8,128)} %all-reduce.10.cloned.1.call-done) | copy-start | bytes 1376260
Sparse Core Ops, SparseCore 0:
  10.3 61.3 all-reduce.5
  75.0 197.9 all-reduce.7
  310.9 188.5 all-reduce.9
  502.5 49.7 all-reduce.11
where the time goes:
time: 564 us; the launch traced here: 563 us
  waiting for transfers between devices  478 us (85%)
  blocking collectives  48.4 us (9%)
  matrix products  17.8 us (3%)
  between operations  14.5 us (3%)
    psum x1, waiting for transfers between devices, shards(): subspace = lax.psum(local_sub, 'dp')  186 us
    psum x1, waiting for transfers between devices, shards(): proj_grad = lax.psum(local_grad, 'dp')  183 us
    psum x1, waiting for transfers between devices, shards(): summed = lax.psum(partial_value, 'shard')  61.5 us
    psum x1, waiting for transfers between devices, shards(): gram_matrix = lax.psum(gram_local, 'shard')  47.5 us
    psum x1, blocking collectives, shards(): token_scores = lax.psum(score_terms, 'shard').astype(jnp.bfloat16)  33.3 us
    all_gather x1, blocking collectives, shards(): all_rows = lax.all_gather(projector, 'shard', axis=0, tiled=True)  15 us
  transfers between devices with their start and end apart: 4, of which 4 were waited for; matrix products, arithmetic and copies ran while one was open for 1% of the time, Pallas kernels for 0%

commit v1 on v0

--- a/solution.py
+++ b/solution.py
@@ -18,7 +18,7 @@
     score_terms = jnp.einsum("tf,rf->tr", grad_out, proj_low, preferred_element_type=jnp.float32)
     token_scores = lax.psum(score_terms, "shard").astype(jnp.bfloat16)
     local_sub = jnp.einsum("td,tr->dr", acts, token_scores, preferred_element_type=jnp.float32)
-    subspace = lax.psum(local_sub, "dp")
+    subspace = jnp.sum(lax.all_gather(local_sub, "dp"), axis=0)
     gram_local = jnp.dot(
         subspace.T, subspace, precision=lax.Precision.HIGHEST, preferred_element_type=jnp.float32
     )

time: 564 us -> 592 us (1.050)
  other arithmetic: 4.02 us -> 21.4 us
  waiting for transfers between devices: 478 us -> 493 us
    psum x1 -> x0, waiting for transfers between devices: 186 us -> none  [shards(): subspace = lax.psum(local_sub, 'dp')]
    all_gather x0 -> x1, waiting for transfers between devices: none -> 184 us  [shards(): subspace = jnp.sum(lax.all_gather(local_sub, 'dp'), axis=0)]
    reduce_sum x0 -> x1, other arithmetic: none -> 18.5 us  [shards(): subspace = jnp.sum(lax.all_gather(local_sub, 'dp'), axis=0)]
    psum x1, waiting for transfers between devices: 183 us -> 198 us  [shards(): proj_grad = lax.psum(local_grad, 'dp')]
  transfers between devices with their start and end apart: 4 -> 4, of which waited for: 4 -> 4; matrix products, arithmetic and copies ran while one was open for 1% -> 0% of each run, Pallas kernels for 0% -> 0%
where the time goes in v1:
time: 592 us
  waiting for transfers between devices  493 us (83%)
  blocking collectives  47 us (8%)
  other arithmetic  21.4 us (4%)
  matrix products  15.5 us (3%)
  between operations  14.5 us (2%)
    psum x1, waiting for transfers between devices, shards(): proj_grad = lax.psum(local_grad, 'dp')  198 us
    all_gather x1, waiting for transfers between devices, shards(): subspace = jnp.sum(lax.all_gather(local_sub, 'dp'), axis=0)  184 us
    psum x1, waiting for transfers between devices, shards(): summed = lax.psum(partial_value, 'shard')  61.6 us
    psum x1, waiting for transfers between devices, shards(): gram_matrix = lax.psum(gram_local, 'shard')  49.4 us
    psum x1, blocking collectives, shards(): token_scores = lax.psum(score_terms, 'shard').astype(jnp.bfloat16)  33.4 us
    reduce_sum x1, other arithmetic, shards(): subspace = jnp.sum(lax.all_gather(local_sub, 'dp'), axis=0)  18.5 us
    all_gather x1, blocking collectives, shards(): all_rows = lax.all_gather(projector, 'shard', axis=0, tiled=True)  13.6 us
  transfers between devices with their start and end apart: 4, of which 4 were waited for; matrix products, arithmetic and copies ran while one was open for 0% of the time, Pallas kernels for 0%

profile of v1, /device:TPU:8, one launch (start us, length us, event | category | flops | bytes accessed | tf_op | source)
XLA Modules:
  0.0 591.7 jit_solution(18061671478976616150)
XLA Ops:
  7.2 0.0 copy-start
  7.2 0.0 all-reduce.5.cloned.1.call-start
  7.2 2.9 fusion.22
  10.1 0.0 all-reduce.5.cloned.1.call-update
  10.1 0.0 all-reduce.7.cloned.1.call-start
  10.2 61.6 %all-reduce.5.cloned.1.call-done = f32[1024,256]{1,0:T(8,128)} async-done(((f32[1024,256]{1,0:T(8,128)}), f32[1024,256]{1,0:T(8,128)}) %all-reduce.5.cloned.1.call-update) | async-done | bytes 1048592 | tf_op jit(solution)/shard_map/psum | solution.py:13
  71.7 0.0 copy-done
  71.7 2.9 fusion.7
  74.7 0.0 all-reduce.7.cloned.1.call-update
  74.7 0.0 all-gather.3.cloned.1.call-start
  74.7 198.3 %all-reduce.7.cloned.1.call-done = f32[256,896]{1,0:T(8,128)} async-done(((f32[256,896]{1,0:T(8,128)}), f32[256,896]{1,0:T(8,128)}) %all-reduce.7.cloned.1.call-update) | async-done | bytes 917520 | tf_op jit(solution)/shard_map/psum | solution.py:16
  273.0 1.9 convolution_bitcast_fusion
  274.9 0.0 copy-start.3
  275.0 33.4 %all-reduce.10 = bf16[1024,256]{0,1:T(8,128)(2,1)S(1)} all-reduce(f32[1024,256]{0,1:T(8,128)S(1)} %convolution_bitcast_fusion), channel_id=1, replica_groups=mesh['dp'=128,'shard'=4] {'shard'}, use_global_device_ids=true, to_apply=%region_2.0 | all-reduce | flops 262144 | bytes 1572864 | tf_op jit(solution)/shard_map/psum | solution.py:19
  308.4 0.0 copy-start.2
  308.4 0.0 copy-start.4
  308.4 0.0 copy-start.5
  308.4 2.5 convolution_bitcast_fusion.1
  311.0 0.0 all-gather.3.cloned.1.call-update
  311.0 0.0 all-reduce.9.cloned.1.call-start
  311.0 0.0 copy-done.3
  311.1 13.6 %all_gather.11 = bf16[1792,256]{1,0:T(8,128)(2,1)S(1)} all-gather(bf16[448,256]{1,0:T(8,128)(2,1)S(1)} %copy-done.3), channel_id=1, replica_groups=mesh['dp'=128,'shard'=4] {'shard'}, dimensions={0}, use_global_device_ids=true | all-gather | bytes 1146880 | tf_op jit(solution)/shard_map/all_gather | solution.py:42
  324.6 0.0 copy-done.2
  324.6 0.0 copy-done.4
  324.6 0.0 copy-done.5
  324.6 1.4 fusion.4
  326.0 183.8 %all-gather.3.cloned.1.call-done = f32[57344,256]{1,0:T(8,128)} async-done(((f32[448,256]{1,0:T(8,128)}), f32[57344,256]{1,0:T(8,128)}) %all-gather.3.cloned.1.call-update) | async-done | bytes 58720272 | tf_op jit(solution)/shard_map/all_gather | solution.py:21
  509.8 18.5 %reduce_sum.19 = f32[448,256]{1,0:T(8,128)S(1)} reduce(f32[128,448,256]{2,1,0:T(8,128)} %bitcast.15, f32[]{:T(128)} %constant.21.clone.1), dimensions={0}, to_apply=%region_3.0 | reduce | flops 14565376 | bytes 59179012 | tf_op jit(solution)/shard_map/reduce_sum | solution.py:21
  528.2 1.7 fusion.23
  530.0 0.0 all-reduce.9.cloned.1.call-update
  530.0 1.2 fusion.10
  531.2 49.4 %all-reduce.9.cloned.1.call-done = f32[256,256]{1,0:T(8,128)} async-done(((f32[256,256]{1,0:T(8,128)}), f32[256,256]{1,0:T(8,128)}) %all-reduce.9.cloned.1.call-update) | async-done | bytes 262160 | tf_op jit(solution)/shard_map/psum | solution.py:25
  580.6 0.0 copy-start.1
  580.6 1.7 select_reduce_fusion
  583.0 2.2 fusion.3
  585.2 0.0 copy-done.1
Async XLA Ops:
  7.2 64.6 %copy-start = (bf16[1024,896]{1,0:T(8,128)(2,1)S(1)}, bf16[1024,896]{1,0:T(8,128)(2,1)}, u32[]{:S(2)}) copy-start(bf16[1024,896]{1,0:T(8,128)(2,1)} %param.6) | copy-start | bytes 5505028
  7.2 64.5 %all-reduce.5.cloned.1.call-start = ((), (), s32[]{:S(2)}) async-start(), calls=%async_computation | async-start | bytes 2097152 | tf_op jit(solution)/shard_map/psum | solution.py:13
  10.1 262.9 %all-reduce.7.cloned.1.call-start = ((), (), s32[]{:S(2)}) async-start(), calls=%async_computation.1 | async-start | bytes 1835008 | tf_op jit(solution)/shard_map/psum | solution.py:16
  74.7 435.1 %all-gather.3.cloned.1.call-start = ((), (), s32[]{:S(2)}) async-start(), calls=%async_computation.3 | async-start | bytes 59179008 | tf_op jit(solution)/shard_map/all_gather | solution.py:21
  274.9 36.1 %copy-start.3 = (bf16[448,256]{1,0:T(8,128)(2,1)S(1)}, bf16[448,256]{1,0:T(8,128)(2,1)}, u32[]{:S(2)}) copy-start(bf16[448,256]{1,0:T(8,128)(2,1)} %param.7) | copy-start | bytes 688132
  308.4 16.2 %copy-start.2 = (f32[256,896]{1,0:T(8,128)S(1)}, f32[256,896]{1,0:T(8,128)}, u32[]{:S(2)}) copy-start(f32[256,896]{1,0:T(8,128)} %all-reduce.7.cloned.1.call-done) | copy-start | bytes 2752516
  308.4 16.2 %copy-start.4 = (bf16[256,896]{1,0:T(8,128)(2,1)S(1)}, bf16[256,896]{1,0:T(8,128)(2,1)}, u32[]{:S(2)}) copy-start(bf16[256,896]{1,0:T(8,128)(2,1)} %param.9) | copy-start | bytes 1376260
  308.4 16.2 %copy-start.5 = (bf16[256,896]{1,0:T(8,128)(2,1)S(1)}, bf16[256,896]{1,0:T(8,128)(2,1)}, u32[]{:S(2)}) copy-start(bf16[256,896]{1,0:T(8,128)(2,1)} %param.8) | copy-start | bytes 1376260
  311.0 269.6 %all-reduce.9.cloned.1.call-start = ((), (), s32[]{:S(2)}) async-start(), calls=%async_computation.2 | async-start | bytes 524288 | tf_op jit(solution)/shard_map/psum | solution.py:25
  580.6 4.6 copy-start.1
Sparse Core Ops, SparseCore 0:
  10.3 61.3 all-reduce.4
  75.0 197.9 all-reduce.6
  311.1 198.6 all-gather.2
  530.1 50.4 all-reduce.8
